TPU v7x, 32 devices: a whole 2x2x4 slice. The times are simulated.
32 devices in a mesh: wide: 8 (over z, x), narrow: 4 (over y, core).
Axes of the slice: x: 2, y: 2, z: 4, core: 2. Of those that a mesh axis runs over, the one named last changes fastest.
Arguments:
- tokens: bfloat16 [26880, 768], P(('wide', 'narrow')), may hold values from -6 to 6
- patch_counts: int32 [96], P('wide'), may hold values from 100 to 240, as said below
- ln1_gain: float32 [768], replicated, may hold values from 0.25 to 1.75
- ln1_bias: float32 [768], replicated, may hold values from -3 to 3
- w_qkv: bfloat16 [768, 3, 768], P(None, None, 'narrow'), may hold values from -0.21875 to 0.21875
- b_qv: float32 [2, 768], P(None, 'narrow'), may hold values from -3 to 3
- w_out: bfloat16 [768, 768], P('narrow'), may hold values from -0.625 to 0.625
- b_out: float32 [768], replicated, may hold values from -3 to 3
- ln2_gain: float32 [768], replicated, may hold values from 0.25 to 1.75
- ln2_bias: float32 [768], replicated, may hold values from -3 to 3
- w_up: bfloat16 [768, 3072], P(None, 'narrow'), may hold values from -0.21875 to 0.21875
- b_up: bfloat16 [1, 3072], P(None, 'narrow'), may hold values from -3 to 3
- w_down: bfloat16 [3072, 768], P('narrow'), may hold values from -0.109375 to 0.109375
- b_down: float32 [768], replicated, may hold values from -3 to 3
- cotangent: bfloat16 [26880, 768], P(('wide', 'narrow')), may hold values from -6 to 6
Outputs:
- layer_out: float32 [26880, 768], P(('wide', 'narrow'))
- input_grad: float32 [26880, 768], P(('wide', 'narrow'))
- ln1_gain_grad: float32 [768], replicated
- ln1_bias_grad: float32 [768], replicated
- w_qkv_grad: float32 [768, 3, 768], P(None, None, 'narrow')
- b_qv_grad: float32 [2, 768], P(None, 'narrow')
- w_out_grad: float32 [768, 768], P('narrow')
- b_out_grad: float32 [768], replicated
- ln2_gain_grad: float32 [768], replicated
- ln2_bias_grad: float32 [768], replicated
- w_up_grad: float32 [768, 3072], P(None, 'narrow')
- b_up_grad: float32 [1, 3072], P(None, 'narrow')
- w_down_grad: float32 [3072, 768], P('narrow')
- b_down_grad: float32 [768], replicated
Inputs may be any that keep to these rules, and one draw needn't show every extreme that they name: patch_counts[i] is the number of real patches of item i; key positions 40 + patch_counts[i] and later of that item are padding.
All inputs are finite; a program needn't handle non-finite values.
Results may differ from a plain program's by a relative error of at most 0.012.
The roundings to bfloat16 on the way count: a program that leaves them out, or rounds other values in their place, can miss the bound.
Values may be sent and summed in bfloat16 or wider, within the bound.
No kernel may reach another device: no remote copies, remote signals or barrier semaphores. Data moves between devices by JAX's collectives and lax.ppermute only.
A program may use at most 192 MiB of HBM per device.

v0:
```python
import jax
import jax.numpy as jnp
from jax import lax
from jax.sharding import PartitionSpec as P

HEAD = 64
WORDS = 40
norm_eps = 1e-06
masked_value = -1000000000.0


def norm_parts(inputs, gain_row, bias_row):
    mean_rows = jnp.mean(inputs, axis=-1, keepdims=True)
    centred = inputs - mean_rows
    var_rows = jnp.mean(centred * centred, axis=-1, keepdims=True)
    inv_scale = lax.rsqrt(var_rows + norm_eps)
    unit_rows = centred * inv_scale
    return (unit_rows * gain_row + bias_row, unit_rows, inv_scale)


def norm_back(grad_rows, unit_rows, inv_scale, gain_row):
    scaled = grad_rows * gain_row
    inner = (
        scaled
        - jnp.mean(scaled, axis=-1, keepdims=True)
        - unit_rows * jnp.mean(scaled * unit_rows, axis=-1, keepdims=True)
    )
    return (inv_scale * inner, jnp.sum(grad_rows * unit_rows, axis=0), jnp.sum(grad_rows, axis=0))


def contract_rows(left_side, right_side):
    return lax.dot_general(
        left_side, right_side, (((0,), (0,)), ((), ())), preferred_element_type=jnp.float32
    )


def contract_cols(left_side, right_side):
    return lax.dot_general(
        left_side, right_side, (((1,), (1,)), ((), ())), preferred_element_type=jnp.float32
    )


def gelu_exact(inputs):
    return jax.nn.gelu(inputs, approximate=False)


def on_device(
    tokens,
    patch_counts,
    ln1_gain,
    ln1_bias,
    w_qkv,
    b_qv,
    w_out,
    b_out,
    ln2_gain,
    ln2_bias,
    w_up,
    b_up,
    w_down,
    b_down,
    cotangent,
):
    inputs = tokens.astype(jnp.float32)
    normed1, unit1, inv1 = norm_parts(inputs, ln1_gain, ln1_bias)
    normed1 = normed1.astype(jnp.bfloat16)
    grouped = lax.all_gather(normed1, "narrow", axis=0, tiled=True)
    full_out, full_down = (
        lax.all_gather(w_out, "narrow", axis=0, tiled=True),
        lax.all_gather(w_down, "narrow", axis=0, tiled=True),
    )
    full_up, full_up_bias = (
        lax.all_gather(w_up, "narrow", axis=1, tiled=True),
        lax.all_gather(b_up, "narrow", axis=1, tiled=True),
    )
    projected = jnp.einsum("td,dcf->tcf", grouped, w_qkv, preferred_element_type=jnp.float32)
    queries = ((projected[:, 0] + b_qv[0]) * 0.125).astype(jnp.bfloat16)
    key_rows = projected[:, 1].astype(jnp.bfloat16)
    value_rows = (projected[:, 2] + b_qv[1]).astype(jnp.bfloat16)
    item_count = patch_counts.shape[0]
    head_cols = w_qkv.shape[2]
    group_rows = grouped.shape[0]
    seq_len = group_rows // item_count
    shaped = (item_count, seq_len, head_cols // HEAD, HEAD)
    query_four = queries.reshape(shaped)
    key_four = key_rows.reshape(shaped)
    value_four = value_rows.reshape(shaped)
    positions = jnp.arange(seq_len)
    valid_keys = positions[None, :] < (WORDS + patch_counts)[:, None]
    key_mask = jnp.where(valid_keys, 0.0, masked_value).astype(jnp.float32)[:, None, None, :]
    scores = (
        jnp.einsum("iqhe,ikhe->ihqk", query_four, key_four, preferred_element_type=jnp.float32)
        + key_mask
    )
    row_max = jnp.max(scores, axis=-1, keepdims=True)
    shifted = jnp.exp(scores - row_max)
    row_total = jnp.sum(shifted, axis=-1, keepdims=True)
    log_total = row_max + jnp.log(row_total)
    weights = (shifted / row_total).astype(jnp.bfloat16)
    mixed = jnp.einsum("ihqk,ikhe->iqhe", weights, value_four, preferred_element_type=jnp.float32)
    mixed = mixed.astype(jnp.bfloat16).reshape(group_rows, head_cols)
    regrouped = lax.all_to_all(mixed, "narrow", split_axis=0, concat_axis=1, tiled=True)
    middle = inputs + (jnp.dot(regrouped, full_out, preferred_element_type=jnp.float32) + b_out)
    normed2, unit2, inv2 = norm_parts(middle, ln2_gain, ln2_bias)
    normed2 = normed2.astype(jnp.bfloat16)
    up_rows = jnp.dot(normed2, full_up, preferred_element_type=jnp.float32) + full_up_bias.astype(
        jnp.float32
    )
    activated, gelu_back = jax.vjp(gelu_exact, up_rows)
    hidden = activated.astype(jnp.bfloat16)
    layer_out = middle + jnp.dot(hidden, full_down, preferred_element_type=jnp.float32) + b_down
    grad_float = cotangent.astype(jnp.float32)
    grad_hidden = contract_cols(cotangent, full_down)
    grad_up = gelu_back(grad_hidden)[0].astype(jnp.bfloat16)
    grad_normed2 = contract_cols(grad_up, full_up)
    grad_norm_two, gain2_grad, bias2_grad = norm_back(grad_normed2, unit2, inv2, ln2_gain)
    grad_middle = grad_float + grad_norm_two
    grad_branch = grad_middle.astype(jnp.bfloat16)
    grad_mixed = contract_cols(grad_branch, full_out).astype(jnp.bfloat16)
    grad_heads = lax.all_to_all(grad_mixed, "narrow", split_axis=1, concat_axis=0, tiled=True)
    grad_four = grad_heads.reshape(shaped)
    scores_again = (
        jnp.einsum("iqhe,ikhe->ihqk", query_four, key_four, preferred_element_type=jnp.float32)
        + key_mask
    )
    prob_rows = jnp.exp(scores_again - log_total)
    weights_again = prob_rows.astype(jnp.bfloat16)
    grad_values = jnp.einsum(
        "ihqk,iqhe->ikhe", weights_again, grad_four, preferred_element_type=jnp.float32
    ).astype(jnp.bfloat16)
    grad_probs = jnp.einsum(
        "iqhe,ikhe->ihqk", grad_four, value_four, preferred_element_type=jnp.float32
    )
    grad_scores = (
        prob_rows * (grad_probs - jnp.sum(grad_probs * prob_rows, axis=-1, keepdims=True))
    ).astype(jnp.bfloat16)
    grad_queries = jnp.einsum(
        "ihqk,ikhe->iqhe", grad_scores, key_four, preferred_element_type=jnp.float32
    ).astype(jnp.bfloat16)
    grad_keys = jnp.einsum(
        "ihqk,iqhe->ikhe", grad_scores, query_four, preferred_element_type=jnp.float32
    ).astype(jnp.bfloat16)
    grad_queries = grad_queries.reshape(group_rows, head_cols) * 0.125
    grad_keys = grad_keys.reshape(group_rows, head_cols)
    grad_values = grad_values.reshape(group_rows, head_cols)
    grad_qkv = jnp.stack([grad_queries, grad_keys, grad_values], axis=1)
    w_qkv_grad = jnp.einsum("td,tcf->dcf", grouped, grad_qkv, preferred_element_type=jnp.float32)
    b_qv_grad = jnp.stack(
        [
            jnp.sum(grad_queries.astype(jnp.float32), axis=0),
            jnp.sum(grad_values.astype(jnp.float32), axis=0),
        ]
    )
    full_qkv = lax.all_gather(w_qkv, "narrow", axis=2, tiled=True)
    grad_qkv_own = lax.all_to_all(grad_qkv, "narrow", split_axis=0, concat_axis=2, tiled=True)
    grad_normed1 = jnp.einsum(
        "tcf,dcf->td", grad_qkv_own, full_qkv, preferred_element_type=jnp.float32
    )
    grad_norm_one, gain1_grad, bias1_grad = norm_back(grad_normed1, unit1, inv1, ln1_gain)
    input_grad = grad_middle + grad_norm_one
    out_bias_grad = jnp.sum(grad_branch.astype(jnp.float32), axis=0)
    down_bias_grad = jnp.sum(grad_float, axis=0)
    up_bias_full = jnp.sum(grad_up.astype(jnp.float32), axis=0, keepdims=True)
    out_whole = contract_rows(regrouped, grad_branch)
    down_whole = contract_rows(hidden, cotangent)
    out_part, down_part = (
        lax.psum_scatter(
            out_whole.astype(jnp.bfloat16), "narrow", scatter_dimension=0, tiled=True
        ).astype(jnp.float32),
        lax.psum_scatter(
            down_whole.astype(jnp.bfloat16), "narrow", scatter_dimension=0, tiled=True
        ).astype(jnp.float32),
    )
    up_whole = contract_rows(normed2, grad_up)
    up_part = lax.psum_scatter(
        up_whole.astype(jnp.bfloat16), "narrow", scatter_dimension=1, tiled=True
    ).astype(jnp.float32)
    summed = lax.psum((w_qkv_grad, b_qv_grad, out_part, up_part, down_part), "wide")
    small = lax.psum(
        (
            gain1_grad,
            bias1_grad,
            out_bias_grad,
            gain2_grad,
            bias2_grad,
            down_bias_grad,
            up_bias_full,
        ),
        ("wide", "narrow"),
    )
    shard_cols = b_up.shape[1]
    up_bias_grad = lax.dynamic_slice_in_dim(
        small[6], lax.axis_index("narrow") * shard_cols, shard_cols, 1
    )
    return (
        layer_out,
        input_grad,
        small[0],
        small[1],
        summed[0],
        summed[1],
        summed[2],
        small[2],
        small[3],
        small[4],
        summed[3],
        up_bias_grad,
        summed[4],
        small[5],
    )


def solution(mesh):
    placed = (
        P(("wide", "narrow"), None),
        P("wide"),
        P(),
        P(),
        P(None, None, "narrow"),
        P(None, "narrow"),
        P("narrow", None),
        P(),
        P(),
        P(),
        P(None, "narrow"),
        P(None, "narrow"),
        P("narrow", None),
        P(),
        P(("wide", "narrow"), None),
    )
    return jax.shard_map(
        on_device,
        mesh=mesh,
        in_specs=placed,
        out_specs=(
            P(("wide", "narrow"), None),
            P(("wide", "narrow"), None),
            P(),
            P(),
            P(None, None, "narrow"),
            P(None, "narrow"),
            P("narrow", None),
            P(),
            P(),
            P(),
            P(None, "narrow"),
            P(None, "narrow"),
            P("narrow", None),
            P(),
        ),
        check_vma=False,
    )
```

profile of v0, /device:TPU:0, one launch (start us, length us, event | category | flops | bytes accessed | tf_op | source)
XLA Modules:
  0.0 726.5 jit_solution(6485242681903960717)
XLA Ops:
  16.6 40.5 %all-gather.6.cloned.1.call-done = bf16[3360,768]{1,0:T(8,128)(2,1)} async-done(((bf16[840,768]{1,0:T(8,128)(2,1)}), bf16[3360,768]{1,0:T(8,128)(2,1)}) %all-gather.6.cloned.1.call-update) | async-done | bytes 5160976 | tf_op jit(solution)/shard_map/all_gather | solution.py:67
  57.1 5.5 fusion.47
  66.5 5.4 squeeze.8
  89.2 6.3 add_reduce_fusion
  101.7 5.6 convert_bitcast_fusion.2
  119.2 29.1 %all_gather.21 = bf16[1,3072]{1,0:T(2,128)(2,1)S(1)} all-gather(bf16[1,768]{1,0:T(2,128)(2,1)S(1)} %copy-done.34), channel_id=1, replica_groups=mesh['wide'=8,'narrow'=4] {'narrow'}, dimensions={1}, use_global_device_ids=true | all-gather | bytes 7680 | tf_op jit(solution)/shard_map/all_gather | solution.py:74
  153.6 11.5 %fusion.43 = f32[840,3072]{1,0:T(8,128)} fusion(bf16[768,3072]{1,0:T(8,128)(2,1)} %all-gather.10.cloned.1.call-done, f32[840,768]{1,0:T(8,128)} %copy-done.8, f32[768]{0:T(1024)S(1)} %copy-done.38, f32[768]{0:T(1024)S(1)} %copy-done.33, f32[840]{0:T(1024)S(1)} %add_rsqrt_fusion, f32[840]{0:T(1024)S(1)} %broadcast_multiply_fusion.4), kind=kOutput, calls=%fused_computation.104 | convolution fusion | flops 3966842880 | bytes 17633856 | tf_op jit(solution)/shard_map/dot_general | solution.py:106
  165.1 31.9 %convert_reduce_fusion = (f32[3072]{0:T(1024)S(1)}, bf16[840,3072]{1,0:T(8,128)(2,1)S(1)}, f32[840,3072]{1,0:T(8,128)}) fusion(f32[840,3072]{1,0:T(8,128)} %fusion.43, f32[3072]{0:T(1024)S(1)} %bitcast.79, bf16[840,768]{1,0:T(8,128)(2,1)S(1)} %copy-done.17, bf16[3072,768]{1,0:T(8,128)(2,1)} %all-gather.12.cloned.1.call-done), kind=kOutput, calls=%fused_computation.9 | convolution fusion | flops 4157150208 | bytes 31838208 | tf_op jit(solution)/shard_map/dot_general | solution.py:38
  206.3 9.9 %convolution_convert_fusion.1 = bf16[768,3072]{1,0:T(8,128)(2,1)} fusion(bf16[840,3072]{1,0:T(8,128)(2,1)} %copy-done.42, f32[840,768]{1,0:T(8,128)} %copy-done.8, f32[768]{0:T(1024)S(1)} %copy-done.39, f32[768]{0:T(1024)S(1)} %copy-done.33, f32[840]{0:T(1024)S(1)} %add_rsqrt_fusion, f32[840]{0:T(1024)S(1)} %broadcast_multiply_fusion.4), kind=kOutput, calls=%fused_computation.31 | convolution fusion | flops 3969202176 | bytes 12472896 | tf_op jit(solution)/shard_map/dot_general | solution.py:32
  226.9 12.0 %multiply_convert_fusion.1 = bf16[840,3072]{1,0:T(8,128)(2,1)} fusion(f32[840,3072]{1,0:T(8,128)} %get-tuple-element.37, f32[840,3072]{1,0:T(8,128)} %fusion.43, f32[3072]{0:T(1024)S(1)} %bitcast.80), kind=kLoop, calls=%fused_computation.11 | loop fusion | flops 10321920 | bytes 25817088 | tf_op jit(solution)/shard_map/convert_element_type | solution.py:110
  238.9 10.3 %convolution_convert_fusion = bf16[3072,768]{1,0:T(8,128)(2,1)} fusion(bf16[840,3072]{1,0:T(8,128)(2,1)} %multiply_convert_fusion.1, bf16[840,768]{1,0:T(8,128)(2,1)S(1)} %copy-done.19), kind=kOutput, calls=%fused_computation.30 | convolution fusion | flops 3965976576 | bytes 11169792 | tf_op jit(solution)/shard_map/dot_general | solution.py:32
  255.3 16.3 %multiply_reduce_fusion = (f32[12,3,280]{2,1,0:T(4,128)S(1)}, f32[12,3,280,280]{2,3,1,0:T(8,128)}) fusion(f32[12,3,280,280]{2,3,1,0:T(8,128)} %copy-done, f32[12,3,280]{2,1,0:T(4,128)S(1)} %log_add_fusion, f32[12,280]{1,0:T(8,128)S(1)} %copy-done.22, bf16[12,280,3,64]{1,0,3,2:T(8,128)(2,1)} %add_convert_fusion.1, bf16[12,280,3,64]{1,0,3,2:T(8,128)(2,1)S(1)} %reshape.150), kind=kOutput, calls=%fused_computation.2 | convolution fusion | flops 372546720 | bytes 25253760 | tf_op jit(solution)/shard_map/iqhe,ikhe->ihqk/dot_general | solution.py:131
  271.6 13.6 %multiply_convert_fusion = bf16[12,3,280,280]{2,3,1,0:T(8,128)(2,1)S(1)} fusion(f32[12,3,280,280]{2,3,1,0:T(8,128)} %get-tuple-element.49, f32[12,3,280,280]{2,3,1,0:T(8,128)} %copy-done, f32[12,3,280]{2,1,0:T(4,128)S(1)} %get-tuple-element.48, f32[12,3,280]{2,1,0:T(4,128)S(1)} %log_add_fusion, f32[12,280]{1,0:T(8,128)S(1)} %copy-done.22), kind=kLoop, calls=%fused_computation.1 | loop fusion | flops 14112000 | bytes 28318080 | tf_op jit(solution)/shard_map/convert_element_type | solution.py:136
  295.7 6.6 convert_bitcast_fusion.1
  309.2 7.3 %convert_reduce_fusion.2 = (f32[3,64]{1,0:T(4,128)S(1)}, bf16[12,280,3,64]{1,3,2,0:T(8,128)(2,1)S(1)}) fusion(f32[12,3,280,280]{2,3,1,0:T(8,128)} %copy-done, f32[12,3,280]{2,1,0:T(4,128)S(1)} %log_add_fusion, f32[12,280]{1,0:T(8,128)S(1)} %copy-done.22, bf16[12,280,3,64]{1,0,3,2:T(8,128)(2,1)S(1)} %reshape.150), kind=kOutput, calls=%fused_computation.37 | convolution fusion | flops 371669568 | bytes 13924608 | tf_op jit(solution)/shard_map/ihqk,iqhe->ikhe/dot_general | solution.py:128
  325.3 11.3 %copy.78 = bf16[3360,3,192]{2,1,0:T(4,128)(2,1)} copy(bf16[3360,3,192]{0,2,1:T(8,128)(2,1)} %constant_dynamic-update-slice_fusion) | data formatting | bytes 7741440 | tf_op jit(solution)/shard_map/stack | solution.py:146
  336.6 5.6 all-to-all-start.2
  342.5 9.5 %add_add_fusion = f32[840,768]{1,0:T(8,128)} fusion(f32[840,768]{1,0:T(8,128)S(1)} %copy-done.10, bf16[840,3072]{1,0:T(8,128)(2,1)} %multiply_convert_fusion.1, bf16[3072,768]{1,0:T(8,128)(2,1)} %all-gather.12.cloned.1.call-done, f32[768]{0:T(1024)S(1)} %copy-done.40), kind=kOutput, calls=%fused_computation.61 | convolution fusion | flops 3964907520 | bytes 15043584 | tf_op jit(solution)/shard_map/dot_general | solution.py:111
  352.2 8.2 %fusion.48 = f32[768,576]{0,1} fusion(bf16[3360,576]{0,1:T(8,128)(2,1)} %bitcast.15, bf16[3360,768]{1,0:T(8,128)(2,1)} %all-gather.6.cloned.1.call-done), kind=kOutput, calls=%fused_computation.108 | convolution fusion | flops 2972712960 | bytes 10801152
  360.5 78.4 %all-to-all-done.2 = bf16[3360,3,192]{2,1,0:T(4,128)(2,1)} async-done(((bf16[3360,3,192]{2,1,0:T(4,128)(2,1)}), bf16[3360,3,192]{2,1,0:T(4,128)(2,1)}, u32[]{:S(2)}, u32[]{:S(2)}) %all-to-all-start.2) | async-done | bytes 3870752 | tf_op jit(solution)/shard_map/all_to_all | solution.py:155
  439.0 11.4 %copy.79 = bf16[4,840,3,192]{1,3,0,2:T(8,128)(2,1)} copy(bf16[4,840,3,192]{3,2,1,0:T(4,128)(2,1)} %bitcast.11) | data formatting | bytes 7741440 | tf_op jit(solution)/shard_map/all_to_all | solution.py:155
  450.4 8.6 %fusion.25 = (f32[768]{0:T(1024)S(1)}, f32[840]{0:T(1024)S(1)}, f32[840]{0:T(1024)S(1)}, f32[768]{0:T(1024)S(1)}, f32[840,768,1]{1,0,2:T(8,128)}) fusion(bf16[840,768]{1,0:T(8,128)(2,1)S(1)} %copy-done.3, f32[840]{0:T(1024)S(1)} %copy-done.31, f32[840]{0:T(1024)S(1)} %copy-done.29, f32[768]{0:T(1024)S(1)} %copy-done.32, bf16[840,3,768]{0,2,1:T(8,128)(2,1)} %bitcast.74, ...), kind=kOutput, calls=%fused_computation.54 | convolution fusion | flops 2979161088 | bytes 11303040 | tf_op jit(solution)/shard_map/tcf,dcf->td/dot_general | solution.py:156
  458.9 41.5 %all-reduce = (f32[768]{0:T(1024)}, f32[768]{0:T(1024)}, f32[768]{0:T(1024)}, f32[768]{0:T(1024)}, f32[768]{0:T(1024)}, /*index=5*/f32[1,3072]{1,0:T(1,128)S(1)}, f32[768]{0:T(1024)}) all-reduce(f32[768]{0:T(1024)S(1)} %get-tuple-element.16, f32[768]{0:T(1024)S(1)} %get-tuple-element.21, ...), channel_id=1, replica_groups=mesh['wide'=8,'narrow'=4] {'wide','narrow'}, use_global_device_ids=true, to_apply=%region_12.13 | all-reduce | flops 7680 | bytes 61440 | tf_op jit(solution)/shard_map/psum | solution.py:179
  505.1 211.7 %all-reduce.6 = (f32[2,192]{1,0:T(2,128)}, f32[192,768]{1,0:T(8,128)}, f32[768,768]{1,0:T(8,128)}, f32[768,768]{1,0:T(8,128)}) all-reduce(f32[2,192]{1,0:T(2,128)S(1)} %pad_maximum_fusion, bf16[192,768]{1,0:T(8,128)(2,1)S(1)} %copy-done.27, ...), channel_id=1, replica_groups=mesh['wide'=8,'narrow'=4] {'wide'}, use_global_device_ids=true, to_apply=%region_18.19 | all-reduce | flops 1327488 | bytes 7965696 | tf_op jit(solution)/shard_map/psum | solution.py:178
  (168 shorter events, 113.5 us)
Async XLA Ops:
  7.2 49.9 %all-gather.6.cloned.1.call-start = ((), (), s32[]{:S(2)}) async-start(), calls=%async_computation.6 | async-start | bytes 6451200 | tf_op jit(solution)/shard_map/all_gather | solution.py:67
  10.7 46.4 %copy-start.20 = (bf16[768,3,192]{0,2,1:T(8,128)(2,1)S(1)}, bf16[768,3,192]{0,2,1:T(8,128)(2,1)}, u32[]{:S(2)}) copy-start(bf16[768,3,192]{0,2,1:T(8,128)(2,1)} %param.19) | copy-start | bytes 2654212
  14.2 134.1 %all-gather.8.cloned.1.call-start = ((), (), s32[]{:S(2)}) async-start(), calls=%async_computation.7 | async-start | bytes 1474560 | tf_op jit(solution)/shard_map/all_gather | solution.py:69
  15.0 138.6 %all-gather.10.cloned.1.call-start = ((), (), s32[]{:S(2)}) async-start(), calls=%async_computation.8 | async-start | bytes 5898240 | tf_op jit(solution)/shard_map/all_gather | solution.py:73
  15.7 149.4 %all-gather.12.cloned.1.call-start = ((), (), s32[]{:S(2)}) async-start(), calls=%async_computation.9 | async-start | bytes 5898240 | tf_op jit(solution)/shard_map/all_gather | solution.py:70
  16.4 82.5 %copy-start.21 = (f32[12,280]{1,0:T(8,128)}, f32[12,280]{1,0:T(8,128)S(1)}, u32[]{:S(2)}) copy-start(f32[12,280]{1,0:T(8,128)S(1)} %fusion.40) | copy-start | bytes 40324
  112.9 35.5 %copy-start.2 = (bf16[840,768]{1,0:T(8,128)(2,1)S(1)}, bf16[840,768]{1,0:T(8,128)(2,1)}, u32[]{:S(2)}) copy-start(bf16[840,768]{1,0:T(8,128)(2,1)} %param.15) | copy-start | bytes 3870724
  112.9 35.5 %copy-start.37 = (f32[768]{0:T(1024)S(1)}, f32[768]{0:T(1024)}, u32[]{:S(2)}) copy-start(f32[768]{0:T(1024)} %param.22) | copy-start | bytes 9220
  115.6 32.8 %all-to-all-start = ((bf16[4,840,192]{1,2,0:T(8,128)(2,1)}), bf16[4,840,192]{1,2,0:T(8,128)(2,1)S(1)}, u32[]{:S(2)}, u32[]{:S(2)}) async-start(bf16[4,840,192]{1,2,0:T(8,128)(2,1)} %copy.64), calls=%async_computation | async-start | bytes 2752512 | tf_op jit(solution)/shard_map/all_to_all | solution.py:102
  119.1 241.4 %reduce-scatter.4.cloned.1.call-start = ((), (), s32[]{:S(2)}) async-start(), calls=%async_computation.12 | async-start | bytes 1474560 | tf_op jit(solution)/shard_map/reduce_scatter | solution.py:167
  153.6 11.5 %copy-start.17 = (bf16[840,768]{1,0:T(8,128)(2,1)S(1)}, bf16[840,768]{1,0:T(8,128)(2,1)}, u32[]{:S(2)}) copy-start(bf16[840,768]{1,0:T(8,128)(2,1)} %param.29) | copy-start | bytes 3870724
  165.1 31.9 %copy-start.9 = (f32[840,768]{1,0:T(8,128)S(1)}, f32[840,768]{1,0:T(8,128)}, u32[]{:S(2)}) copy-start(f32[840,768]{1,0:T(8,128)} %copy-done.8) | copy-start | bytes 7741444
  165.1 31.9 %copy-start.36 = (bf16[768,3072]{1,0:T(8,128)(2,1)S(1)}, bf16[768,3072]{1,0:T(8,128)(2,1)}, u32[]{:S(2)}) copy-start(bf16[768,3072]{1,0:T(8,128)(2,1)} %all-gather.10.cloned.1.call-done) | copy-start | bytes 14155780
  203.2 14.0 %copy-start.7 = (f32[840,768]{1,0:T(8,128)}, f32[840,768]{1,0:T(8,128)S(1)}, u32[]{:S(2)}) copy-start(f32[840,768]{1,0:T(8,128)S(1)} %get-tuple-element.39) | copy-start | bytes 7741444
  205.7 244.7 %all-gather.14.cloned.1.call-start = ((), (), s32[]{:S(2)}) async-start(), calls=%async_computation.10 | async-start | bytes 4423680 | tf_op jit(solution)/shard_map/all_gather | solution.py:154
  206.2 298.8 %reduce-scatter.6.cloned.1.call-start = ((), (), s32[]{:S(2)}) async-start(), calls=%async_computation.13 | async-start | bytes 5898240 | tf_op jit(solution)/shard_map/reduce_scatter | solution.py:175
  223.3 26.0 %all-to-all-start.1 = ((bf16[840,4,192]{0,2,1:T(8,128)(2,1)}), bf16[840,4,192]{0,2,1:T(8,128)(2,1)S(1)}, u32[]{:S(2)}, u32[]{:S(2)}) async-start(bf16[840,4,192]{0,2,1:T(8,128)(2,1)} %bitcast.6), calls=%async_computation.1 | async-start | bytes 2752512 | tf_op jit(solution)/shard_map/all_to_all | solution.py:120
  226.8 278.2 %reduce-scatter.8.cloned.1.call-start = ((), (), s32[]{:S(2)}) async-start(), calls=%async_computation.14 | async-start | bytes 5898240 | tf_op jit(solution)/shard_map/reduce_scatter | solution.py:170
  226.9 12.0 %copy-start.19 = (bf16[840,768]{1,0:T(8,128)(2,1)S(1)}, bf16[840,768]{1,0:T(8,128)(2,1)}, u32[]{:S(2)}) copy-start(bf16[840,768]{1,0:T(8,128)(2,1)} %param.29) | copy-start | bytes 3870724
  271.6 13.7 %copy-start.5 = (bf16[12,280,3,64]{1,0,3,2:T(8,128)(2,1)S(1)}, bf16[12,280,3,64]{1,0,3,2:T(8,128)(2,1)}, u32[]{:S(2)}) copy-start(bf16[12,280,3,64]{1,0,3,2:T(8,128)(2,1)} %copy-done.4) | copy-start | bytes 3870724
  336.6 102.4 %all-to-all-start.2 = ((bf16[3360,3,192]{2,1,0:T(4,128)(2,1)}), bf16[3360,3,192]{2,1,0:T(4,128)(2,1)}, u32[]{:S(2)}, u32[]{:S(2)}) async-start(bf16[3360,3,192]{2,1,0:T(4,128)(2,1)} %copy.78), calls=%async_computation.2 | async-start | bytes 13762560 | tf_op jit(solution)/shard_map/all_to_all | solution.py:155
  342.2 374.5 %all-reduce.5.cloned.1.call-start = ((), (), s32[]{:S(2)}) async-start(), calls=%async_computation.11 | async-start | bytes 3538944 | tf_op jit(solution)/shard_map/psum | solution.py:178
  439.0 11.4 %copy-start.31 = (f32[840]{0:T(1024)S(1)}, f32[840]{0:T(1024)}, u32[]{:S(2)}) copy-start(f32[840]{0:T(1024)} %copy-done.30) | copy-start | bytes 10084
  439.0 11.4 %copy-start.32 = (f32[768]{0:T(1024)S(1)}, f32[768]{0:T(1024)}, u32[]{:S(2)}) copy-start(f32[768]{0:T(1024)} %param.17) | copy-start | bytes 9220
  (31 other events, 144.4 us)
Sparse Core Ops, SparseCore 0:
  14.3 42.6 all-gather.5
  58.6 17.4 all-gather.7
  77.7 37.4 all-gather.9
  116.6 47.4 all-gather.11
  205.8 25.8 reduce-scatter.3
  233.2 32.4 all-gather.13
  268.3 47.8 reduce-scatter.5
  318.7 67.6 reduce-scatter.7
  391.0 94.6 all-reduce.4
where the time goes:
time: 738 us; the launch traced here: 727 us
  blocking collectives  282 us (38%)
  matrix products  154 us (21%)
  waiting for transfers between devices  121 us (16%)
  local copies, waits for them, and re-layouts  93.5 us (13%)
  other arithmetic  47.4 us (6%)
  between operations  14.9 us (2%)
  starting transfers between devices  13.3 us (2%)
    psum x1, blocking collectives, on_device(): lax.psum((w_qkv_grad, b_qv_grad, out_part, up_part, down_part), 'wide')  212 us
    all_to_all x1, waiting for transfers between devices, on_device(): lax.all_to_all(grad_qkv, 'narrow', split_axis=0, concat_axis=2, tiled=True)  78.4 us
    psum x1, blocking collectives, on_device(): lax.psum((gain1_grad, bias1_grad, out_bias_grad, gain2_grad, bias2_grad,...  41.5 us
    all_gather x1, waiting for transfers between devices, on_device(): grouped = lax.all_gather(normed1, 'narrow', axis=0, tiled=True)  40.5 us
    dot_general x3, matrix products, contract_cols(): lax.dot_general(left_side, right_side, (((1,), (1,)), ((), ())), preferre...  40.2 us
    all_gather x1, blocking collectives, on_device(): lax.all_gather(b_up, 'narrow', axis=1, tiled=True)  29.1 us
    dot_general x3, matrix products, contract_rows(): lax.dot_general(left_side, right_side, (((0,), (0,)), ((), ())), preferre...  22.7 us
    another operation x4, local copies, waits for them, and re-layouts, on_device(): grad_qkv = jnp.stack([grad_queries, grad_keys, grad_values], axis=1)  19.5 us
  transfers between devices with their start and end apart: 12, of which 2 were waited for; matrix products, arithmetic and copies ran while one was open for 32% of the time, Pallas kernels for 0%

commit v1 on v0

--- a/solution.py
+++ b/solution.py
@@ -152,7 +152,12 @@
         ]
     )
     full_qkv = lax.all_gather(w_qkv, "narrow", axis=2, tiled=True)
-    grad_qkv_own = lax.all_to_all(grad_qkv, "narrow", split_axis=0, concat_axis=2, tiled=True)
+    grad_qkv_own = jnp.concatenate(
+        lax.all_to_all(
+            jnp.stack(jnp.split(grad_qkv, lax.axis_size("narrow"), axis=0)), "narrow", 0, 0
+        ),
+        axis=2,
+    )
     grad_normed1 = jnp.einsum(
         "tcf,dcf->td", grad_qkv_own, full_qkv, preferred_element_type=jnp.float32
     )

time: 738 us -> 705 us (0.955)
  waiting for transfers between devices: 121 us -> 97.4 us
  local copies, waits for them, and re-layouts: 93.5 us -> 77 us
    all_to_all x1, waiting for transfers between devices: 78.4 us -> 54.4 us  [on_device(): lax.all_to_all(jnp.stack(jnp.split(grad_qkv, lax.axis_size('narrow'), axi...]
    another operation x4 -> x3, local copies, waits for them, and re-layouts: 19.5 us -> 7.24 us  [on_device(): grad_qkv = jnp.stack([grad_queries, grad_keys, grad_values], axis=1)]
    all_to_all x1 -> x0, local copies, waits for them, and re-layouts: 11.4 us -> none  [on_device(): lax.all_to_all(grad_qkv, 'narrow', split_axis=0, concat_axis=2, tiled=True)]
  transfers between devices with their start and end apart: 12 -> 12, of which waited for: 2 -> 2; matrix products, arithmetic and copies ran while one was open for 32% -> 31% of each run, Pallas kernels for 0% -> 0%
where the time goes in v1:
time: 705 us; the launch traced here: 694 us
  blocking collectives  287 us (41%)
  matrix products  154 us (22%)
  waiting for transfers between devices  97.4 us (14%)
  local copies, waits for them, and re-layouts  77 us (11%)
  other arithmetic  50.1 us (7%)
  between operations  14.9 us (2%)
  starting transfers between devices  13 us (2%)
    psum x1, blocking collectives, on_device(): lax.psum((w_qkv_grad, b_qv_grad, out_part, up_part, down_part), 'wide')  216 us
    all_to_all x1, waiting for transfers between devices, on_device(): lax.all_to_all(jnp.stack(jnp.split(grad_qkv, lax.axis_size('narrow'), axi...  54.4 us
    psum x1, blocking collectives, on_device(): lax.psum((gain1_grad, bias1_grad, out_bias_grad, gain2_grad, bias2_grad,...  40.7 us
    all_gather x1, waiting for transfers between devices, on_device(): grouped = lax.all_gather(normed1, 'narrow', axis=0, tiled=True)  40.5 us
    dot_general x3, matrix products, contract_cols(): lax.dot_general(left_side, right_side, (((1,), (1,)), ((), ())), preferre...  40.2 us
    all_gather x1, blocking collectives, on_device(): lax.all_gather(b_up, 'narrow', axis=1, tiled=True)  30.5 us
    dot_general x3, matrix products, contract_rows(): lax.dot_general(left_side, right_side, (((0,), (0,)), ((), ())), preferre...  23.2 us
    dot_general x1, matrix products, on_device(): jnp.einsum('iqhe,ikhe->ihqk', grad_four, value_four, preferred_element_ty...  16.4 us
  transfers between devices with their start and end apart: 12, of which 2 were waited for; matrix products, arithmetic and copies ran while one was open for 31% of the time, Pallas kernels for 0%

profile of v1, /device:TPU:0, one launch (start us, length us, event | category | flops | bytes accessed | tf_op | source)
XLA Modules:
  0.0 694.0 jit_solution(14273363866613842925)
XLA Ops:
  16.6 40.5 %all-gather.6.cloned.1.call-done = bf16[3360,768]{1,0:T(8,128)(2,1)} async-done(((bf16[840,768]{1,0:T(8,128)(2,1)}), bf16[3360,768]{1,0:T(8,128)(2,1)}) %all-gather.6.cloned.1.call-update) | async-done | bytes 5160976 | tf_op jit(solution)/shard_map/all_gather | solution.py:67
  57.1 5.5 fusion.47
  66.6 5.4 squeeze.8
  89.3 6.3 add_reduce_fusion
  101.8 5.6 convert_bitcast_fusion.2
  120.7 30.5 %all_gather.21 = bf16[1,3072]{1,0:T(2,128)(2,1)S(1)} all-gather(bf16[1,768]{1,0:T(2,128)(2,1)S(1)} %copy-done.34), channel_id=1, replica_groups=mesh['wide'=8,'narrow'=4] {'narrow'}, dimensions={1}, use_global_device_ids=true | all-gather | bytes 7680 | tf_op jit(solution)/shard_map/all_gather | solution.py:74
  156.6 11.5 %fusion.43 = f32[840,3072]{1,0:T(8,128)} fusion(bf16[768,3072]{1,0:T(8,128)(2,1)} %all-gather.10.cloned.1.call-done, f32[840,768]{1,0:T(8,128)} %copy-done.8, f32[768]{0:T(1024)S(1)} %copy-done.38, f32[768]{0:T(1024)S(1)} %copy-done.33, f32[840]{0:T(1024)S(1)} %add_rsqrt_fusion, f32[840]{0:T(1024)S(1)} %broadcast_multiply_fusion.4), kind=kOutput, calls=%fused_computation.109 | convolution fusion | flops 3966842880 | bytes 17633856 | tf_op jit(solution)/shard_map/dot_general | solution.py:106
  168.1 31.8 %convert_reduce_fusion = (f32[3072]{0:T(1024)S(1)}, bf16[840,3072]{1,0:T(8,128)(2,1)S(1)}, f32[840,3072]{1,0:T(8,128)}) fusion(f32[840,3072]{1,0:T(8,128)} %fusion.43, f32[3072]{0:T(1024)S(1)} %bitcast.86, bf16[840,768]{1,0:T(8,128)(2,1)S(1)} %copy-done.17, bf16[3072,768]{1,0:T(8,128)(2,1)} %all-gather.12.cloned.1.call-done), kind=kOutput, calls=%fused_computation.9 | convolution fusion | flops 4157150208 | bytes 31838208 | tf_op jit(solution)/shard_map/dot_general | solution.py:38
  200.0 4.7 multiply_reduce_fusion.1
  209.3 10.3 %convolution_convert_fusion.1 = bf16[768,3072]{1,0:T(8,128)(2,1)} fusion(bf16[840,3072]{1,0:T(8,128)(2,1)} %copy-done.42, f32[840,768]{1,0:T(8,128)} %copy-done.8, f32[768]{0:T(1024)S(1)} %copy-done.39, f32[768]{0:T(1024)S(1)} %copy-done.33, f32[840]{0:T(1024)S(1)} %add_rsqrt_fusion, f32[840]{0:T(1024)S(1)} %broadcast_multiply_fusion.4), kind=kOutput, calls=%fused_computation.31 | convolution fusion | flops 3969202176 | bytes 12472896 | tf_op jit(solution)/shard_map/dot_general | solution.py:32
  230.4 12.0 %multiply_convert_fusion.1 = bf16[840,3072]{1,0:T(8,128)(2,1)} fusion(f32[840,3072]{1,0:T(8,128)} %get-tuple-element.37, f32[840,3072]{1,0:T(8,128)} %fusion.43, f32[3072]{0:T(1024)S(1)} %bitcast.87), kind=kLoop, calls=%fused_computation.11 | loop fusion | flops 10321920 | bytes 25817088 | tf_op jit(solution)/shard_map/convert_element_type | solution.py:110
  242.4 10.4 %convolution_convert_fusion = bf16[3072,768]{1,0:T(8,128)(2,1)} fusion(bf16[840,3072]{1,0:T(8,128)(2,1)} %multiply_convert_fusion.1, bf16[840,768]{1,0:T(8,128)(2,1)S(1)} %copy-done.19), kind=kOutput, calls=%fused_computation.30 | convolution fusion | flops 3965976576 | bytes 11169792 | tf_op jit(solution)/shard_map/dot_general | solution.py:32
  258.8 16.4 %multiply_reduce_fusion = (f32[12,3,280]{2,1,0:T(4,128)S(1)}, f32[12,3,280,280]{2,3,1,0:T(8,128)}) fusion(f32[12,3,280,280]{2,3,1,0:T(8,128)} %copy-done, f32[12,3,280]{2,1,0:T(4,128)S(1)} %log_add_fusion, f32[12,280]{1,0:T(8,128)S(1)} %copy-done.22, bf16[12,280,3,64]{1,0,3,2:T(8,128)(2,1)} %add_convert_fusion.1, bf16[12,280,3,64]{1,0,3,2:T(8,128)(2,1)S(1)} %reshape.156), kind=kOutput, calls=%fused_computation.2 | convolution fusion | flops 372546720 | bytes 25253760 | tf_op jit(solution)/shard_map/iqhe,ikhe->ihqk/dot_general | solution.py:131
  275.2 13.7 %multiply_convert_fusion = bf16[12,3,280,280]{2,3,1,0:T(8,128)(2,1)S(1)} fusion(f32[12,3,280,280]{2,3,1,0:T(8,128)} %get-tuple-element.53, f32[12,3,280,280]{2,3,1,0:T(8,128)} %copy-done, f32[12,3,280]{2,1,0:T(4,128)S(1)} %get-tuple-element.52, f32[12,3,280]{2,1,0:T(4,128)S(1)} %log_add_fusion, f32[12,280]{1,0:T(8,128)S(1)} %copy-done.22), kind=kLoop, calls=%fused_computation.1 | loop fusion | flops 14112000 | bytes 28318080 | tf_op jit(solution)/shard_map/convert_element_type | solution.py:136
  299.3 6.6 convert_bitcast_fusion.1
  312.8 7.2 %convert_reduce_fusion.2 = (f32[3,64]{1,0:T(4,128)S(1)}, bf16[12,280,3,64]{1,3,2,0:T(8,128)(2,1)S(1)}) fusion(f32[12,3,280,280]{2,3,1,0:T(8,128)} %copy-done, f32[12,3,280]{2,1,0:T(4,128)S(1)} %log_add_fusion, f32[12,280]{1,0:T(8,128)S(1)} %copy-done.22, bf16[12,280,3,64]{1,0,3,2:T(8,128)(2,1)S(1)} %reshape.156), kind=kOutput, calls=%fused_computation.38 | convolution fusion | flops 371669568 | bytes 13924608 | tf_op jit(solution)/shard_map/ihqk,iqhe->ikhe/dot_general | solution.py:128
  331.7 5.1 all-to-all-start.2
  337.1 9.6 %add_add_fusion = f32[840,768]{1,0:T(8,128)} fusion(f32[840,768]{1,0:T(8,128)S(1)} %copy-done.10, bf16[840,3072]{1,0:T(8,128)(2,1)} %multiply_convert_fusion.1, bf16[3072,768]{1,0:T(8,128)(2,1)} %all-gather.12.cloned.1.call-done, f32[768]{0:T(1024)S(1)} %copy-done.40), kind=kOutput, calls=%fused_computation.62 | convolution fusion | flops 3964907520 | bytes 15043584 | tf_op jit(solution)/shard_map/dot_general | solution.py:111
  346.9 8.2 %fusion.48 = f32[768,576]{0,1} fusion(bf16[3360,576]{0,1:T(8,128)(2,1)} %bitcast.77, bf16[3360,768]{1,0:T(8,128)(2,1)} %all-gather.6.cloned.1.call-done), kind=kOutput, calls=%fused_computation.113 | convolution fusion | flops 2972712960 | bytes 10801152
  355.2 54.4 %all-to-all-done.2 = bf16[4,840,3,192]{1,3,2,0:T(8,128)(2,1)} async-done(((bf16[4,840,3,192]{1,3,2,0:T(8,128)(2,1)}), bf16[4,840,3,192]{1,3,2,0:T(8,128)(2,1)}, u32[]{:S(2)}, u32[]{:S(2)}) %all-to-all-start.2) | async-done | bytes 3870752 | tf_op jit(solution)/shard_map/all_to_all | solution.py:156
  409.6 4.6 copy.78
  414.2 8.6 %fusion.25 = (f32[768]{0:T(1024)S(1)}, f32[840]{0:T(1024)S(1)}, f32[840]{0:T(1024)S(1)}, f32[768]{0:T(1024)S(1)}, f32[840,768,1]{1,0,2:T(8,128)}) fusion(bf16[840,768]{1,0:T(8,128)(2,1)S(1)} %copy-done.3, f32[840]{0:T(1024)S(1)} %copy-done.31, f32[840]{0:T(1024)S(1)} %copy-done.29, f32[768]{0:T(1024)S(1)} %copy-done.32, bf16[840,3,768]{0,2,1:T(8,128)(2,1)} %bitcast.81, ...), kind=kOutput, calls=%fused_computation.55 | convolution fusion | flops 2979161088 | bytes 11303040 | tf_op jit(solution)/shard_map/tcf,dcf->td/dot_general | solution.py:161
  422.8 40.7 %all-reduce = (f32[768]{0:T(1024)}, f32[768]{0:T(1024)}, f32[768]{0:T(1024)}, f32[768]{0:T(1024)}, f32[768]{0:T(1024)}, /*index=5*/f32[1,3072]{1,0:T(1,128)S(1)}, f32[768]{0:T(1024)}) all-reduce(f32[768]{0:T(1024)S(1)} %get-tuple-element.16, f32[768]{0:T(1024)S(1)} %get-tuple-element.21, ...), channel_id=1, replica_groups=mesh['wide'=8,'narrow'=4] {'wide','narrow'}, use_global_device_ids=true, to_apply=%region_12.13 | all-reduce | flops 7680 | bytes 61440 | tf_op jit(solution)/shard_map/psum | solution.py:184
  468.1 216.1 %all-reduce.6 = (f32[2,192]{1,0:T(2,128)}, f32[192,768]{1,0:T(8,128)}, f32[768,768]{1,0:T(8,128)}, f32[768,768]{1,0:T(8,128)}) all-reduce(f32[2,192]{1,0:T(2,128)S(1)} %pad_maximum_fusion.1, bf16[192,768]{1,0:T(8,128)(2,1)S(1)} %copy-done.27, ...), channel_id=1, replica_groups=mesh['wide'=8,'narrow'=4] {'wide'}, use_global_device_ids=true, to_apply=%region_18.19 | all-reduce | flops 1327488 | bytes 7965696 | tf_op jit(solution)/shard_map/psum | solution.py:183
  (169 shorter events, 113.3 us)
Async XLA Ops:
  7.2 49.9 %all-gather.6.cloned.1.call-start = ((), (), s32[]{:S(2)}) async-start(), calls=%async_computation.6 | async-start | bytes 6451200 | tf_op jit(solution)/shard_map/all_gather | solution.py:67
  8.8 7.7 %copy-start.35 = (f32[2,192]{1,0:T(2,128)S(1)}, f32[2,192]{1,0:T(2,128)}, u32[]{:S(2)}) copy-start(f32[2,192]{1,0:T(2,128)} %param.20) | copy-start | bytes 4612
  8.8 48.3 %copy-start.20 = (bf16[768,3,192]{0,2,1:T(8,128)(2,1)S(1)}, bf16[768,3,192]{0,2,1:T(8,128)(2,1)}, u32[]{:S(2)}) copy-start(bf16[768,3,192]{0,2,1:T(8,128)(2,1)} %param.19) | copy-start | bytes 2654212
  14.3 137.0 %all-gather.8.cloned.1.call-start = ((), (), s32[]{:S(2)}) async-start(), calls=%async_computation.7 | async-start | bytes 1474560 | tf_op jit(solution)/shard_map/all_gather | solution.py:69
  15.1 141.5 %all-gather.10.cloned.1.call-start = ((), (), s32[]{:S(2)}) async-start(), calls=%async_computation.8 | async-start | bytes 5898240 | tf_op jit(solution)/shard_map/all_gather | solution.py:73
  15.8 152.3 %all-gather.12.cloned.1.call-start = ((), (), s32[]{:S(2)}) async-start(), calls=%async_computation.9 | async-start | bytes 5898240 | tf_op jit(solution)/shard_map/all_gather | solution.py:70
  16.5 82.5 %copy-start.21 = (f32[12,280]{1,0:T(8,128)}, f32[12,280]{1,0:T(8,128)S(1)}, u32[]{:S(2)}) copy-start(f32[12,280]{1,0:T(8,128)S(1)} %fusion.40) | copy-start | bytes 40324
  111.4 9.3 %copy-start.34 = (bf16[1,768]{1,0:T(2,128)(2,1)S(1)}, bf16[1,768]{1,0:T(2,128)(2,1)}, u32[]{:S(2)}) copy-start(bf16[1,768]{1,0:T(2,128)(2,1)} %param.26) | copy-start | bytes 4612
  111.4 39.9 %copy-start.2 = (bf16[840,768]{1,0:T(8,128)(2,1)S(1)}, bf16[840,768]{1,0:T(8,128)(2,1)}, u32[]{:S(2)}) copy-start(bf16[840,768]{1,0:T(8,128)(2,1)} %param.15) | copy-start | bytes 3870724
  111.4 39.9 %copy-start.37 = (f32[768]{0:T(1024)S(1)}, f32[768]{0:T(1024)}, u32[]{:S(2)}) copy-start(f32[768]{0:T(1024)} %param.22) | copy-start | bytes 9220
  116.9 34.4 %all-to-all-start = ((bf16[4,840,192]{1,2,0:T(8,128)(2,1)}), bf16[4,840,192]{1,2,0:T(8,128)(2,1)S(1)}, u32[]{:S(2)}, u32[]{:S(2)}) async-start(bf16[4,840,192]{1,2,0:T(8,128)(2,1)} %copy.64), calls=%async_computation | async-start | bytes 2752512 | tf_op jit(solution)/shard_map/all_to_all | solution.py:102
  120.7 234.5 %reduce-scatter.4.cloned.1.call-start = ((), (), s32[]{:S(2)}) async-start(), calls=%async_computation.12 | async-start | bytes 1474560 | tf_op jit(solution)/shard_map/reduce_scatter | solution.py:172
  156.5 11.6 %copy-start.17 = (bf16[840,768]{1,0:T(8,128)(2,1)S(1)}, bf16[840,768]{1,0:T(8,128)(2,1)}, u32[]{:S(2)}) copy-start(bf16[840,768]{1,0:T(8,128)(2,1)} %param.29) | copy-start | bytes 3870724
  168.1 31.8 %copy-start.9 = (f32[840,768]{1,0:T(8,128)S(1)}, f32[840,768]{1,0:T(8,128)}, u32[]{:S(2)}) copy-start(f32[840,768]{1,0:T(8,128)} %copy-done.8) | copy-start | bytes 7741444
  168.1 31.8 %copy-start.36 = (bf16[768,3072]{1,0:T(8,128)(2,1)S(1)}, bf16[768,3072]{1,0:T(8,128)(2,1)}, u32[]{:S(2)}) copy-start(bf16[768,3072]{1,0:T(8,128)(2,1)} %all-gather.10.cloned.1.call-done) | copy-start | bytes 14155780
  206.1 14.4 %copy-start.7 = (f32[840,768]{1,0:T(8,128)}, f32[840,768]{1,0:T(8,128)S(1)}, u32[]{:S(2)}) copy-start(f32[840,768]{1,0:T(8,128)S(1)} %get-tuple-element.39) | copy-start | bytes 7741444
  208.7 205.5 %all-gather.14.cloned.1.call-start = ((), (), s32[]{:S(2)}) async-start(), calls=%async_computation.10 | async-start | bytes 4423680 | tf_op jit(solution)/shard_map/all_gather | solution.py:154
  209.2 258.9 %reduce-scatter.6.cloned.1.call-start = ((), (), s32[]{:S(2)}) async-start(), calls=%async_computation.13 | async-start | bytes 5898240 | tf_op jit(solution)/shard_map/reduce_scatter | solution.py:180
  226.8 26.0 %all-to-all-start.1 = ((bf16[840,4,192]{0,2,1:T(8,128)(2,1)}), bf16[840,4,192]{0,2,1:T(8,128)(2,1)S(1)}, u32[]{:S(2)}, u32[]{:S(2)}) async-start(bf16[840,4,192]{0,2,1:T(8,128)(2,1)} %bitcast.6), calls=%async_computation.1 | async-start | bytes 2752512 | tf_op jit(solution)/shard_map/all_to_all | solution.py:120
  230.3 237.8 %reduce-scatter.8.cloned.1.call-start = ((), (), s32[]{:S(2)}) async-start(), calls=%async_computation.14 | async-start | bytes 5898240 | tf_op jit(solution)/shard_map/reduce_scatter | solution.py:175
  230.4 12.0 %copy-start.19 = (bf16[840,768]{1,0:T(8,128)(2,1)S(1)}, bf16[840,768]{1,0:T(8,128)(2,1)}, u32[]{:S(2)}) copy-start(bf16[840,768]{1,0:T(8,128)(2,1)} %param.29) | copy-start | bytes 3870724
  275.2 13.7 %copy-start.5 = (bf16[12,280,3,64]{1,0,3,2:T(8,128)(2,1)S(1)}, bf16[12,280,3,64]{1,0,3,2:T(8,128)(2,1)}, u32[]{:S(2)}) copy-start(bf16[12,280,3,64]{1,0,3,2:T(8,128)(2,1)} %copy-done.4) | copy-start | bytes 3870724
  331.7 77.9 %all-to-all-start.2 = ((bf16[4,840,3,192]{1,3,2,0:T(8,128)(2,1)}), bf16[4,840,3,192]{1,3,2,0:T(8,128)(2,1)}, u32[]{:S(2)}, u32[]{:S(2)}) async-start(bf16[4,840,3,192]{1,3,2,0:T(8,128)(2,1)} %pad_maximum_fusion), calls=%async_computation.2 | async-start | bytes 8257536 | tf_op jit(solution)/shard_map/all_to_all | solution.py:156
  336.8 347.4 %all-reduce.5.cloned.1.call-start = ((), (), s32[]{:S(2)}) async-start(), calls=%async_computation.11 | async-start | bytes 3538944 | tf_op jit(solution)/shard_map/psum | solution.py:183
  (31 other events, 127.5 us)
Sparse Core Ops, SparseCore 0:
  14.4 42.6 all-gather.5
  58.7 17.4 all-gather.7
  77.7 37.4 all-gather.9
  116.7 48.8 all-gather.11
  208.8 25.5 reduce-scatter.3
  235.9 32.8 all-gather.13
  271.5 47.6 reduce-scatter.5
  321.8 73.2 reduce-scatter.7
  399.6 108.7 all-reduce.4
